TPU v7x, 128 devices: a whole 4x4x4 slice. The times are simulated.
128 devices in a mesh: wide: 16 (over y, x), narrow: 8 (over z, core).
Axes of the slice: x: 4, y: 4, z: 4, core: 2. Of those that a mesh axis runs over, the one named last changes fastest.
Arguments:
- old_fields: float32 [1024, 3, 32768], P(('wide', 'narrow')), may hold values from -6 to 6
- old_source: float32 [1024, 3, 32768], P(('wide', 'narrow')), may hold values from -12 to 12
- old_kappa: float32 [1024, 32768], P(('wide', 'narrow')), may hold values from 0.05 to 4
- patch_ids: int32 [1024], P(('wide', 'narrow')), may hold values from -1 to 511, as said below
Outputs:
- solution: float32 [3, 256, 512, 128], P(None, 'narrow', 'wide')
Inputs may be any that keep to these rules, and one draw needn't show every extreme that they name: `patch_ids`: every patch number of 0 to 511 stands in exactly one slot, on a device with the same index of narrow as the device whose block of solution holds its box. From the slots of one device at most 2 patches go to the block of any one device, and exactly 2 to some device in every index of narrow. The block of every device receives exactly 4 patches. In every index of narrow some device has all its 8 slots filled and another none.
All inputs are finite; a program needn't handle non-finite values.
Results may differ from a plain program's by a relative error of at most 0.00002.
Values sent between devices are 32-bit elements; how exact they have to be, the bound alone decides.
A program may use at most 256 MiB of HBM per device.

v0:
```python
import jax
import jax.numpy as jnp
from jax import lax
from jax.sharding import PartitionSpec as P

PS = 32
BXR = 1
BYD = 1
BZ = 4
SWEEPS = 3
CAP = 2
K = 4
LX = 32
LY = 32
LZ = 128


OMEGA = 1.5


def with_halo(array, sides, width):
    for axis, dim in sides:
        size, length = (lax.axis_size(axis), array.shape[dim])
        up = [(i, (i + 1) % size) for i in range(size - 1)]
        down = [(j, i) for i, j in up]
        last = lax.slice_in_dim(array, length - width, length, axis=dim)
        leading = lax.slice_in_dim(array, 0, width, axis=dim)
        before = lax.ppermute(last, axis, up)
        after = lax.ppermute(leading, axis, down)
        array = jnp.concatenate([before, array, after], axis=dim)
    return array


def six_sum(values):
    widths = [(0, 0)] * (values.ndim - 3) + [(1, 1)] * 3
    padded = jnp.pad(values, widths)
    return (
        padded[..., 2:, 1:-1, 1:-1]
        + padded[..., :-2, 1:-1, 1:-1]
        + padded[..., 1:-1, 2:, 1:-1]
        + padded[..., 1:-1, :-2, 1:-1]
        + padded[..., 1:-1, 1:-1, 2:]
        + padded[..., 1:-1, 1:-1, :-2]
    )


def relax_once(current, source, inverse, selected):
    padded = with_halo(current, (("wide", 2), ("narrow", 1)), 1)
    beside_all = six_sum(padded)[:, 1:-1, 1:-1, :]
    update = current + OMEGA * ((source + beside_all) * inverse - current)
    return jnp.where(selected, update, current)


def local(old_fields, old_source, old_kappa, patch_ids):
    cell_count = old_kappa.shape[1]
    wide_count = lax.axis_size("wide")
    capacity = CAP
    boxes_wide = wide_count * BYD
    occupied = patch_ids >= 0
    depth_box = patch_ids % BZ
    wide_box = patch_ids // BZ % boxes_wide
    high_box = patch_ids // (BZ * boxes_wide)
    target_dev = wide_box // BYD
    new_slot = (high_box % BXR * BYD + wide_box % BYD) * BZ + depth_box
    onehot = (
        (target_dev[:, None] == jnp.arange(wide_count, dtype=jnp.int32)[None, :])
        & occupied[:, None]
    ).astype(jnp.int32)
    before = jnp.cumsum(onehot, axis=0) - onehot
    rank_in = jnp.sum(before * onehot, axis=1)
    position = jnp.where(occupied, target_dev * capacity + rank_in, wide_count * capacity)
    payload = jnp.concatenate([old_fields, old_source, old_kappa[:, None, :]], axis=1)
    outgoing = (
        jnp.zeros((wide_count * capacity, 7, cell_count), jnp.float32)
        .at[position]
        .set(payload, mode="drop")
    )
    labels = (
        jnp.full((wide_count * capacity,), -1.0, jnp.float32)
        .at[position]
        .set(new_slot.astype(jnp.float32), mode="drop")
    )
    arrived, arrived_labels = (
        lax.all_to_all(outgoing, "wide", split_axis=0, concat_axis=0, tiled=True),
        lax.all_to_all(labels, "wide", split_axis=0, concat_axis=0, tiled=True),
    )
    slot_index = arrived_labels.astype(jnp.int32)
    slot_index = jnp.where(slot_index >= 0, slot_index, K)
    placed = jnp.zeros((K, 7, cell_count), jnp.float32).at[slot_index].set(arrived, mode="drop")
    blocks = (
        placed.reshape(BXR, BYD, BZ, 7, PS, PS, PS)
        .transpose(3, 0, 4, 1, 5, 2, 6)
        .reshape(7, LX, LY, LZ)
    )
    current = blocks[0:3]
    source = blocks[3:6]
    inverse = 1.0 / (6.0 + blocks[6])
    coord_z = jnp.arange(LZ, dtype=jnp.int32)[None, None, :]
    coord_x = jnp.arange(LX, dtype=jnp.int32)[:, None, None]
    coord_y = jnp.arange(LY, dtype=jnp.int32)[None, :, None]
    parity = (coord_x + coord_y + coord_z) % 2
    red_cells = parity == 0
    black_cells = parity == 1
    for sweep_number in range(SWEEPS):
        current = relax_once(
            current, source, inverse, red_cells if sweep_number == 0 else red_cells
        )
        current = relax_once(current, source, inverse, black_cells)
    return current


def solution(mesh):
    in_specs = (
        P(("wide", "narrow"), None, None),
        P(("wide", "narrow"), None, None),
        P(("wide", "narrow"), None),
        P(("wide", "narrow")),
    )
    out_specs = P(None, "narrow", "wide", None)
    return jax.shard_map(local, mesh=mesh, in_specs=in_specs, out_specs=out_specs, check_vma=False)
```

profile of v0, /device:TPU:40, one launch (start us, length us, event | category | flops | bytes accessed | tf_op | source)
XLA Modules:
  0.0 839.5 jit_solution(12338049028350805026)
XLA Ops:
  3.6 7.4 all-to-all-start
  14.4 7.6 copy.18
  22.0 11.0 %broadcast_in_dim.63 = f32[32,7,32768]{2,1,0:T(8,128)} broadcast(f32[]{:T(128)} %constant.101.clone.1), dimensions={} | broadcast | bytes 29360132 | tf_op jit(solution)/shard_map/broadcast_in_dim | solution.py:74
  33.0 12.4 %scatter_fusion = f32[32,7,32768]{2,1,0:T(8,128)} fusion(f32[32,7,32768]{2,1,0:T(8,128)} %broadcast_in_dim.63, s32[8]{0:T(128)S(1)} %get-tuple-element.70, f32[8,7,32768]{2,1,0:T(8,128)} %copy.18), kind=kCustom, calls=%fused_computation.1 | custom fusion | bytes 22020128 | tf_op jit(solution)/shard_map/scatter | solution.py:76
  45.4 10.1 %all-to-all-start.1 = ((f32[32,7,32768]{2,1,0:T(8,128)}), f32[32,7,32768]{2,1,0:T(8,128)}, u32[]{:S(2)}, u32[]{:S(2)}) async-start(f32[32,7,32768]{2,1,0:T(8,128)} %scatter_fusion), calls=%async_computation.1 | async-start | bytes 67108864 | tf_op jit(solution)/shard_map/all_to_all | solution.py:84
  55.6 490.7 %all-to-all-done.1 = f32[32,7,32768]{2,1,0:T(8,128)} async-done(((f32[32,7,32768]{2,1,0:T(8,128)}), f32[32,7,32768]{2,1,0:T(8,128)}, u32[]{:S(2)}, u32[]{:S(2)}) %all-to-all-start.1) | async-done | bytes 29360160 | tf_op jit(solution)/shard_map/all_to_all | solution.py:84
  548.6 42.0 %scatter_fusion.1 = f32[4,7,32768]{2,1,0:T(8,128)} fusion(f32[4,7,32768]{2,1,0:T(8,128)} %broadcast_in_dim.58, s32[32]{0:T(128)S(1)} %fusion.38, f32[32,7,32768]{2,1,0:T(8,128)} %all-to-all-done.1), kind=kCustom, calls=%fused_computation.2 | custom fusion | bytes 88080512 | tf_op jit(solution)/shard_map/scatter | solution.py:89
  590.6 6.3 copy.19
  597.0 9.8 %reshape.63 = f32[1,1,4,7,32,32,32]{6,5,4,2,3,1,0:T(8,128)} reshape(f32[4,7,32768]{2,0,1:T(4,128)} %copy.19) | data formatting | bytes 7340032 | tf_op jit(solution)/shard_map/reshape | solution.py:91
  606.8 8.9 %fusion.41 = (f32[3,1,32,1,32,4,32]{6,4,2,5,0,3,1:T(8,128)}, f32[3,1,32,1,32,4,32]{6,4,2,5,0,3,1:T(8,128)S(1)}) fusion(f32[7,1,32,1,32,4,32]{6,4,2,5,0,3,1:T(8,128)} %bitcast.13), kind=kLoop, calls=%fused_computation.151 | loop fusion | bytes 6291456 | tf_op jit(solution)/shard_map/slice | solution.py:96
  615.7 8.8 %copy.20 = f32[3,1,32,1,32,4,32]{6,5,4,2,0,3,1:T(4,128)} copy(f32[3,1,32,1,32,4,32]{6,4,2,5,0,3,1:T(8,128)S(1)} %get-tuple-element.6) | data formatting | bytes 3145728 | tf_op jit(solution)/shard_map/slice | solution.py:95
  624.4 5.1 slice.215
  631.6 6.0 collective-permute-start.1
  648.9 11.5 %copy.21 = f32[3,1,32,1,32,4,32]{6,5,4,2,0,3,1:T(4,128)} copy(f32[3,1,32,1,32,4,32]{6,4,2,5,0,3,1:T(8,128)} %get-tuple-element.5) | data formatting | bytes 3145728 | tf_op jit(solution)/shard_map/slice | solution.py:96
  660.4 5.3 slice.217
  665.7 4.7 copy.22
  673.5 4.5 select_maximum_fusion.20
  678.0 4.5 fusion.47
  688.2 6.4 collective-permute-start.5
  709.2 4.5 fusion.46
  717.5 6.0 collective-permute-start.8
  740.9 4.5 fusion.45
  800.1 4.5 fusion.43
  834.3 4.9 add_select_fusion
  (89 shorter events, 151.5 us)
Async XLA Ops:
  3.6 41.8 %all-to-all-start = ((f32[16,2,1]{1,2,0:T(1,128)}), f32[16,2,1]{1,2,0:T(1,128)S(1)}, u32[]{:S(2)}, u32[]{:S(2)}) async-start(f32[16,2,1]{1,2,0:T(1,128)} %bitcast), calls=%async_computation | async-start | bytes 16384 | tf_op jit(solution)/shard_map/all_to_all | solution.py:85
  45.4 500.9 %all-to-all-start.1 = ((f32[32,7,32768]{2,1,0:T(8,128)}), f32[32,7,32768]{2,1,0:T(8,128)}, u32[]{:S(2)}, u32[]{:S(2)}) async-start(f32[32,7,32768]{2,1,0:T(8,128)} %scatter_fusion), calls=%async_computation.1 | async-start | bytes 67108864 | tf_op jit(solution)/shard_map/all_to_all | solution.py:84
  629.6 8.4 collective-permute-start
  631.6 7.8 collective-permute-start.1
  640.0 33.4 %collective-permute-start.2 = (f32[3,1,34,128]{3,2,1,0:T(8,128)}, f32[3,1,34,128]{3,2,1,0:T(8,128)}, u32[]{:S(2)}, u32[]{:S(2)}) collective-permute-start(f32[3,1,34,128]{3,2,1,0:T(8,128)} %get-tuple-element.53), channel_id=1, source_target_pairs={{0,1},{1,2},{2,3},{3,4},{4,5},{5,6},{6,7},{8,9},{9,10},{10,11},{11... | collective-permute-start | bytes 156680 | tf_op jit(solution)/shard_map/ppermute | solution.py:28
  641.9 31.5 %collective-permute-start.3 = (f32[3,1,34,128]{3,2,1,0:T(8,128)}, f32[3,1,34,128]{3,2,1,0:T(8,128)}, u32[]{:S(2)}, u32[]{:S(2)}) collective-permute-start(f32[3,1,34,128]{3,2,1,0:T(8,128)} %get-tuple-element.54), channel_id=1, source_target_pairs={{1,0},{2,1},{3,2},{4,3},{5,4},{6,5},{7,6},{9,8},{10,9},{11,10},{12... | collective-permute-start | bytes 156680 | tf_op jit(solution)/shard_map/ppermute | solution.py:29
  686.2 8.4 %collective-permute-start.4 = (f32[3,32,1,128]{3,2,1,0:T(1,128)S(1)}, f32[3,32,1,128]{3,2,1,0:T(1,128)S(1)}, u32[]{:S(2)}, u32[]{:S(2)}) collective-permute-start(f32[3,32,1,128]{3,2,1,0:T(1,128)S(1)} %get-tuple-element.63), channel_id=1, source_target_pairs={{0,8},{8,16},{16,24},{24,32},{32,40},{40,48},{48,56},{56,64},{64,7... | collective-permute-start | bytes 147464 | tf_op jit(solution)/shard_map/ppermute | solution.py:28
  688.2 8.1 collective-permute-start.5
  696.3 5.6 collective-permute-start.6
  699.4 5.9 collective-permute-start.7
  717.5 8.1 collective-permute-start.8
  723.5 6.1 collective-permute-start.9
  729.7 5.6 collective-permute-start.10
  733.3 3.8 collective-permute-start.11
  749.2 8.1 collective-permute-start.12
  753.1 6.0 collective-permute-start.13
  759.1 5.6 collective-permute-start.14
  762.7 3.8 collective-permute-start.15
  778.8 8.2 collective-permute-start.16
  782.8 6.0 collective-permute-start.17
  788.8 5.7 collective-permute-start.18
  808.4 8.1 collective-permute-start.20
  812.3 6.0 collective-permute-start.21
  818.3 5.7 collective-permute-start.22
  (3 other events, 12.0 us)
where the time goes:
time: 851 us; the launch traced here: 839 us
  waiting for transfers between devices  514 us (60%)
  local copies, waits for them, and re-layouts  167 us (20%)
  starting transfers between devices  99.2 us (12%)
  other arithmetic  57.7 us (7%)
    all_to_all x1, waiting for transfers between devices, local(): lax.all_to_all(outgoing, 'wide', split_axis=0, concat_axis=0, tiled=True)  491 us
    scatter x2, local copies, waits for them, and re-layouts, local(): jnp.zeros((K, 7, cell_count), jnp.float32).at[slot_index]  48.3 us
    ppermute x12, starting transfers between devices, with_halo(): before = lax.ppermute(last, axis, up)  41.6 us
    ppermute x12, starting transfers between devices, with_halo(): after = lax.ppermute(leading, axis, down)  40.2 us
    slice x6, local copies, waits for them, and re-layouts, six_sum(): padded[..., 2:, 1:-1, 1:-1] + padded[..., :-2, 1:-1, 1:-1]  26.8 us
    slice x3, local copies, waits for them, and re-layouts, local(): source = blocks[3:6]  25.7 us
    concatenate x6, other arithmetic, with_halo(): array = jnp.concatenate([before, array, after], axis=dim)  23.9 us
    select_n x6, other arithmetic, relax_once(): return jnp.where(selected, update, current)  23.6 us
  transfers between devices with their start and end apart: 26, of which 17 were waited for; matrix products, arithmetic and copies ran while one was open for 7% of the time, Pallas kernels for 0%

commit v1 on v0

v1 whole, which is shorter than its diff:
```python
import jax
import jax.numpy as jnp
from jax import lax
from jax.experimental import pallas as pl
from jax.experimental.pallas import tpu as pltpu
from jax.sharding import PartitionSpec as P

PS = 32
SLOTS = 8
LANES = 128
WIDE = 16
STAGES = 7
CHUNK = 128
PIECE = 64
HALF_SWEEPS = 6
FACE = 96
MESH = pl.DeviceIdType.MESH
F32 = jnp.float32


def row_peer(me, offset):
    row = lax.rem(me // 4 + offset // 4, 4)
    column = lax.rem(lax.rem(me, 4) + lax.rem(offset, 4), 4)
    return row * 4 + column


def kernel(fields, source, kappa, labels, out, *scratch):
    received = scratch[0:STAGES]
    sending = scratch[STAGES : 2 * STAGES]
    (
        cells, rhs, weight, all_labels, start_vmem, start_smem, faces_out, faces_in,
        label_send, label_recv, spread_send, spread_recv, give_send, give_recv,
        own_spread, own_give, start_sem, face_send, face_recv,
    ) = scratch[2 * STAGES :]
    me = lax.axis_index("wide")
    level = lax.axis_index("narrow")
    levels = lax.axis_size("narrow")
    below, above = level > 0, level < levels - 1
    left, right = me > 0, me < WIDE - 1

    faces_in[...] = jnp.zeros_like(faces_in)

    barrier = pltpu.get_barrier_semaphore()

    def greet(offset, carry):
        pl.semaphore_signal(
            barrier, inc=1, device_id=(row_peer(me, offset), level), device_id_type=MESH
        )
        return carry

    lax.fori_loop(1, WIDE, greet, 0)

    @pl.when(below)
    def _():
        pl.semaphore_signal(barrier, inc=1, device_id=(me, level - 1), device_id_type=MESH)

    @pl.when(above)
    def _():
        pl.semaphore_signal(barrier, inc=1, device_id=(me, level + 1), device_id_type=MESH)

    pl.semaphore_wait(
        barrier, WIDE - 1 + below.astype(jnp.int32) + above.astype(jnp.int32)
    )

    def label_copy(target, origin):
        return pltpu.make_async_remote_copy(
            src_ref=labels,
            dst_ref=all_labels.at[pl.ds(origin * SLOTS, SLOTS), :],
            send_sem=label_send.at[target],
            recv_sem=label_recv.at[origin],
            device_id=(target, level),
            device_id_type=MESH,
        )

    def send_label(offset, carry):
        label_copy(row_peer(me, offset), me).start()
        return carry

    lax.fori_loop(1, WIDE, send_label, 0)
    all_labels[pl.ds(me * SLOTS, SLOTS), :] = labels[...]

    def slots_of(stage, part):
        rows = pl.ds(part * CHUNK, CHUNK)
        if stage == 0:
            return kappa.at[rows, :]
        if stage < 4:
            return fields.at[stage - 1, rows, :]
        return source.at[stage - 4, rows, :]

    def spread_copy(stage, target, origin):
        return pltpu.make_async_remote_copy(
            src_ref=slots_of(stage, target),
            dst_ref=received[stage].at[pl.ds(origin * CHUNK, CHUNK), :],
            send_sem=spread_send.at[stage, target],
            recv_sem=spread_recv.at[stage, origin],
            device_id=(target, level),
            device_id_type=MESH,
        )

    def own_spread_copy(stage):
        return pltpu.make_async_copy(
            slots_of(stage, me),
            received[stage].at[pl.ds(me * CHUNK, CHUNK), :],
            own_spread.at[stage],
        )

    for stage in range(STAGES):

        def send_spread(offset, carry):
            spread_copy(stage, row_peer(me, offset), me).start()
            return carry

        lax.fori_loop(1, WIDE, send_spread, 0)
        own_spread_copy(stage).start()

    def wait_label(offset, carry):
        origin = row_peer(me, offset)
        label_copy(origin, origin).wait_recv()
        return carry

    lax.fori_loop(1, WIDE, wait_label, 0)
    slot_row = lax.broadcasted_iota(jnp.int32, (WIDE * SLOTS, LANES), 0)
    wanted = lax.broadcasted_iota(jnp.int32, (WIDE * SLOTS, LANES), 1) + level * (WIDE * 4)
    first = (slot_row // SLOTS) * CHUNK + slot_row % SLOTS
    found = jnp.where(all_labels[...] == wanted, first, 0)
    start_vmem[...] = jnp.max(found, axis=0, keepdims=True)
    move = pltpu.make_async_copy(start_vmem, start_smem, start_sem)
    move.start()
    move.wait()

    lane = lax.broadcasted_iota(jnp.int32, (8, LANES), 1)
    low_half = lane < 64
    low_quarter = lane % 64 < 32

    def place_of(stage, origin):
        if stage == 0:
            return weight.at[pl.ds(origin * PIECE, PIECE), :]
        base = ((stage - 1) % 3) * PS * PS
        home = cells if stage < 4 else rhs
        return home.at[pl.ds(base + origin * PIECE, PIECE), :]

    def give_copy(stage, target, origin):
        return pltpu.make_async_remote_copy(
            src_ref=sending[stage].at[pl.ds(target * PIECE, PIECE), :],
            dst_ref=place_of(stage, origin),
            send_sem=give_send.at[stage, target],
            recv_sem=give_recv.at[stage, origin],
            device_id=(target, level),
            device_id_type=MESH,
        )

    def own_give_copy(stage):
        return pltpu.make_async_copy(
            sending[stage].at[pl.ds(me * PIECE, PIECE), :],
            place_of(stage, me),
            own_give.at[stage],
        )

    for stage in range(STAGES):

        def wait_spread(offset, carry):
            origin = row_peer(me, offset)
            spread_copy(stage, origin, origin).wait_recv()
            return carry

        lax.fori_loop(1, WIDE, wait_spread, 0)
        own_spread_copy(stage).wait()

        def pick(owner, carry):
            starts = [start_smem[0, owner * 4 + part] for part in range(4)]
            for plane in range(2):
                v = [
                    received[stage][pl.ds(start + plane * 64, 8, stride=8), :]
                    for start in starts
                ]
                u = [
                    jnp.where(low_half, v[0], pltpu.roll(v[2], 64, 1)),
                    jnp.where(low_half, v[1], pltpu.roll(v[3], 64, 1)),
                    jnp.where(low_half, pltpu.roll(v[0], 64, 1), v[2]),
                    jnp.where(low_half, pltpu.roll(v[1], 64, 1), v[3]),
                ]
                w = [
                    jnp.where(low_quarter, u[0], pltpu.roll(u[1], 32, 1)),
                    jnp.where(low_quarter, pltpu.roll(u[0], 96, 1), u[1]),
                    jnp.where(low_quarter, u[2], pltpu.roll(u[3], 32, 1)),
                    jnp.where(low_quarter, pltpu.roll(u[2], 96, 1), u[3]),
                ]
                for part in range(4):
                    row = owner * PIECE + plane * PS + part
                    sending[stage][pl.ds(row, 8, stride=4), :] = w[part]
            return carry

        lax.fori_loop(0, WIDE, pick, 0)

        def send_give(offset, carry):
            give_copy(stage, row_peer(me, offset), me).start()
            return carry

        lax.fori_loop(1, WIDE, send_give, 0)
        own_give_copy(stage).start()

    for stage in range(STAGES):

        def wait_give(offset, carry):
            origin = row_peer(me, offset)
            give_copy(stage, origin, origin).wait_recv()
            return carry

        lax.fori_loop(1, WIDE, wait_give, 0)
        own_give_copy(stage).wait()
        if stage == 0:

            def invert(block, carry):
                rows = pl.ds(pl.multiple_of(block * PS, PS), PS)
                weight[rows, :] = 1.5 * (1.0 / (6.0 + weight[rows, :]))
                return carry

            lax.fori_loop(0, PS, invert, 0)

    ways = (
        (above, (me, level + 1), below),
        (below, (me, level - 1), above),
        (right, (me + 1, level), left),
        (left, (me - 1, level), right),
    )

    def face_copy(slot, way):
        return pltpu.make_async_remote_copy(
            src_ref=faces_out.at[slot, way],
            dst_ref=faces_in.at[slot, way],
            send_sem=face_send.at[slot, way],
            recv_sem=face_recv.at[slot, way],
            device_id=ways[way][1],
            device_id_type=MESH,
        )

    row32 = lax.broadcasted_iota(jnp.int32, (PS, LANES), 0)
    lane32 = lax.broadcasted_iota(jnp.int32, (PS, LANES), 1)
    odd = (row32 + lane32) % 2
    first_row, last_row = row32 == 0, row32 == PS - 1
    first_lane, last_lane = lane32 == 0, lane32 == LANES - 1

    for step in range(HALF_SWEEPS):
        slot, colour = step % 2, step % 2
        if step >= 2:
            for way in range(4):

                @pl.when(ways[way][0])
                def _():
                    face_copy(slot, way).wait_send()

        for field in range(3):
            base = field * PS * PS
            faces_out[slot, 0, pl.ds(field * PS, PS), :] = cells[pl.ds(base + (PS - 1) * PS, PS), :]
            faces_out[slot, 1, pl.ds(field * PS, PS), :] = cells[pl.ds(base, PS), :]
        for group in range(FACE // 8):
            rows = pl.ds(group * 8, 8)
            faces_out[slot, 2, rows, :] = cells[pl.ds(group * 8 * PS + PS - 1, 8, stride=PS), :]
            faces_out[slot, 3, rows, :] = cells[pl.ds(group * 8 * PS, 8, stride=PS), :]
        for way in range(4):

            @pl.when(ways[way][0])
            def _():
                face_copy(slot, way).start()

        for way in range(4):

            @pl.when(ways[way][2])
            def _():
                face_copy(slot, way).wait_recv()

        def relax(plane, before_of, after_of):
            mine = (odd + plane) % 2 == colour
            w = weight[pl.ds(pl.multiple_of(plane * PS, PS), PS), :]
            for field in range(3):
                base = pl.multiple_of(field * PS * PS + plane * PS, PS)
                v = cells[pl.ds(base, PS), :]
                line = field * PS + plane
                low = jnp.broadcast_to(faces_in[slot, 2, pl.ds(line, 1), :], (PS, LANES))
                high = jnp.broadcast_to(faces_in[slot, 3, pl.ds(line, 1), :], (PS, LANES))
                total = before_of(field, base) + after_of(field, base)
                total += jnp.where(first_row, low, pltpu.roll(v, 1, 0))
                total += jnp.where(last_row, high, pltpu.roll(v, PS - 1, 0))
                total += jnp.where(first_lane, 0.0, pltpu.roll(v, 1, 1))
                total += jnp.where(last_lane, 0.0, pltpu.roll(v, LANES - 1, 1))
                fresh = (rhs[pl.ds(base, PS), :] + total) * w - 0.5 * v
                fresh = jnp.where(mine, fresh, v)
                if step == HALF_SWEEPS - 1:
                    out[field, plane] = fresh
                else:
                    cells[pl.ds(base, PS), :] = fresh

        def below_face(field, base):
            return faces_in[slot, 0, pl.ds(field * PS, PS), :]

        def above_face(field, base):
            return faces_in[slot, 1, pl.ds(field * PS, PS), :]

        def before(field, base):
            return cells[pl.ds(pl.multiple_of(base - PS, PS), PS), :]

        def after(field, base):
            return cells[pl.ds(pl.multiple_of(base + PS, PS), PS), :]

        relax(0, below_face, after)

        def inner(plane, carry):
            relax(plane, before, after)
            return carry

        lax.fori_loop(1, PS - 1, inner, 0)
        relax(PS - 1, before, above_face)

    for slot in range(2):
        for way in range(4):

            @pl.when(ways[way][0])
            def _():
                face_copy(slot, way).wait_send()

    def drain(offset, carry):
        target = row_peer(me, offset)
        label_copy(target, me).wait_send()
        for stage in range(STAGES):
            spread_copy(stage, target, me).wait_send()
            give_copy(stage, target, me).wait_send()
        return carry

    lax.fori_loop(1, WIDE, drain, 0)


def local(old_fields, old_source, old_kappa, patch_ids):
    def tiles(array):
        lead = array.shape[:-2]
        split = array.reshape(lead + (SLOTS, -1, LANES))
        return jnp.swapaxes(split, -3, -2).reshape(lead + (-1, LANES))

    fields = tiles(jnp.swapaxes(old_fields, 0, 1))
    source = tiles(jnp.swapaxes(old_source, 0, 1))
    kappa = tiles(old_kappa)
    labels = jnp.broadcast_to(patch_ids[:, None], (SLOTS, LANES))
    vmem = pl.BlockSpec(memory_space=pltpu.VMEM)
    anywhere = pl.BlockSpec(memory_space=pl.ANY)
    dma = pltpu.SemaphoreType.DMA
    scratch = (
        [pltpu.VMEM((WIDE * CHUNK, LANES), F32)] * STAGES
        + [pltpu.VMEM((WIDE * PIECE, LANES), F32)] * STAGES
        + [
            pltpu.VMEM((3 * PS * PS, LANES), F32),
            pltpu.VMEM((3 * PS * PS, LANES), F32),
            pltpu.VMEM((PS * PS, LANES), F32),
            pltpu.VMEM((WIDE * SLOTS, LANES), jnp.int32),
            pltpu.VMEM((1, LANES), jnp.int32),
            pltpu.SMEM((1, LANES), jnp.int32),
            pltpu.VMEM((2, 4, FACE, LANES), F32),
            pltpu.VMEM((2, 4, FACE, LANES), F32),
            dma((WIDE,)),
            dma((WIDE,)),
            dma((STAGES, WIDE)),
            dma((STAGES, WIDE)),
            dma((STAGES, WIDE)),
            dma((STAGES, WIDE)),
            dma((STAGES,)),
            dma((STAGES,)),
            dma(()),
            dma((2, 4)),
            dma((2, 4)),
        ]
    )
    return pl.pallas_call(
        kernel,
        out_shape=jax.ShapeDtypeStruct((3, PS, PS, LANES), F32),
        in_specs=[anywhere, anywhere, anywhere, vmem],
        out_specs=vmem,
        scratch_shapes=scratch,
        compiler_params=pltpu.CompilerParams(
            collective_id=0, has_side_effects=True, vmem_limit_bytes=60 << 20
        ),
        name="regrid_and_sweep",
    )(fields, source, kappa, labels)


def solution(mesh):
    in_specs = (
        P(("wide", "narrow"), None, None),
        P(("wide", "narrow"), None, None),
        P(("wide", "narrow"), None),
        P(("wide", "narrow")),
    )
    out_specs = P(None, "narrow", "wide", None)
    return jax.shard_map(local, mesh=mesh, in_specs=in_specs, out_specs=out_specs, check_vma=False)
```

time: 851 us -> 185 us (0.22); the launches traced: 839 us -> 185 us
  waiting for transfers between devices: 514 us -> 0 us
  Pallas kernels: 0 us -> 181 us
  local copies, waits for them, and re-layouts: 167 us -> 3.98 us
  starting transfers between devices: 99.2 us -> 0 us
  other arithmetic: 57.7 us -> 0 us
    all_to_all x2 -> x0, waiting for transfers between devices: 491 us -> none  [the longest x1 491 us: local(): lax.all_to_all(outgoing, 'wide', split_axis=0, concat_axis=0, tiled=True)]
    pallas_call x0 -> x1, Pallas kernels: none -> 181 us  [local(): pl.pallas_call(kernel, out_shape=jax.ShapeDtypeStruct((3, PS, PS, LANES),...]
    ppermute x24 -> x0, starting transfers between devices: 81.8 us -> none  [the longest x12 41.6 us: with_halo(): before = lax.ppermute(last, axis, up)]
    slice x17 -> x0, local copies, waits for them, and re-layouts: 66.8 us -> none  [the longest x6 26.8 us: six_sum(): padded[..., 2:, 1:-1, 1:-1] + padded[..., :-2, 1:-1, 1:-1]]
    scatter x4 -> x0, local copies, waits for them, and re-layouts: 61.3 us -> none  [the longest x2 48.3 us: local(): jnp.zeros((K, 7, cell_count), jnp.float32).at[slot_index]]
    concatenate x7 -> x0, other arithmetic: 27.3 us -> none  [the longest x6 23.9 us: with_halo(): array = jnp.concatenate([before, array, after], axis=dim)]
    select_n x8 -> x0, other arithmetic: 24.2 us -> none  [the longest x6 23.6 us: relax_once(): return jnp.where(selected, update, current)]
    ppermute x24 -> x0, waiting for transfers between devices: 23.8 us -> none  [the longest x12 23.1 us: with_halo(): after = lax.ppermute(leading, axis, down)]
  transfers between devices with their start and end apart: 26 -> 0, of which waited for: 17 -> 0; matrix products, arithmetic and copies ran while one was open for 7% -> 0% of each run, Pallas kernels for 0% -> 0%
where the time goes in v1:
time: 185 us
  Pallas kernels  181 us (98%)
  local copies, waits for them, and re-layouts  3.98 us (2%)
    pallas_call x1, Pallas kernels, local(): pl.pallas_call(kernel, out_shape=jax.ShapeDtypeStruct((3, PS, PS, LANES),...  181 us

profile of v1, /device:TPU:40, one launch (start us, length us, event | category | flops | bytes accessed | tf_op | source)
XLA Modules:
  0.0 184.9 jit_solution(17179304783357371345)
XLA Ops:
  0.0 1.3 broadcast_in_dim.2.labels
  1.3 180.9 %regrid_and_sweep.1 = f32[3,32,32,128]{3,2,1,0:T(8,128)} custom-call(f32[3,2048,128]{2,1,0:T(8,128)} %bitcast.19, f32[3,2048,128]{2,1,0:T(8,128)} %bitcast.20, f32[2048,128]{1,0:T(8,128)} %bitcast.21, s32[8,128]{1,0:T(8,128)} %broadcast_in_dim.2.labels), custom_call_target="tpu_custom_call" | custom-call | tf_op jit(solution)/shard_map/regrid_and_sweep/pallas_call | solution.py:370
  182.2 2.7 %copy.6 = f32[3,32,32,128]{3,2,1,0:T(8,128)} copy(f32[3,32,32,128]{3,2,1,0:T(8,128)} %regrid_and_sweep.1) | data formatting | bytes 3145728

commit v2 on v1

v2 whole, which is shorter than its diff:
```python
import jax
import jax.numpy as jnp
from jax import lax
from jax.experimental import pallas as pl
from jax.experimental.pallas import tpu as pltpu
from jax.sharding import PartitionSpec as P

PS = 32
SLOTS = 8
LANES = 128
WIDE = 16
STAGES = 7
CHUNK = 128
PIECE = 64
HALF_SWEEPS = 6
GROUP = 4
MESH = pl.DeviceIdType.MESH
F32 = jnp.float32


def row_peer(me, offset):
    row = lax.rem(me // 4 + offset // 4, 4)
    column = lax.rem(lax.rem(me, 4) + lax.rem(offset, 4), 4)
    return row * 4 + column


def kernel(fields, source, kappa, labels, out, *scratch):
    received = scratch[0:STAGES]
    sending = scratch[STAGES : 2 * STAGES]
    cells = scratch[2 * STAGES : 2 * STAGES + 3]
    rhs = scratch[2 * STAGES + 3 : 2 * STAGES + 6]
    (
        weight, all_labels, start_vmem, start_smem, faces_out, faces_in,
        label_send, label_recv, spread_send, spread_recv, give_send, give_recv,
        own_spread, own_give, start_sem, face_send, face_recv,
    ) = scratch[2 * STAGES + 6 :]
    me = lax.axis_index("wide")
    level = lax.axis_index("narrow")
    levels = lax.axis_size("narrow")
    below, above = level > 0, level < levels - 1
    left, right = me > 0, me < WIDE - 1

    faces_in[...] = jnp.zeros_like(faces_in)

    barrier = pltpu.get_barrier_semaphore()

    def greet(offset, carry):
        pl.semaphore_signal(
            barrier, inc=1, device_id=(row_peer(me, offset), level), device_id_type=MESH
        )
        return carry

    lax.fori_loop(1, WIDE, greet, 0)

    @pl.when(below)
    def _():
        pl.semaphore_signal(barrier, inc=1, device_id=(me, level - 1), device_id_type=MESH)

    @pl.when(above)
    def _():
        pl.semaphore_signal(barrier, inc=1, device_id=(me, level + 1), device_id_type=MESH)

    pl.semaphore_wait(
        barrier, WIDE - 1 + below.astype(jnp.int32) + above.astype(jnp.int32)
    )

    def label_copy(target, origin):
        return pltpu.make_async_remote_copy(
            src_ref=labels,
            dst_ref=all_labels.at[pl.ds(origin * SLOTS, SLOTS), :],
            send_sem=label_send.at[target],
            recv_sem=label_recv.at[origin],
            device_id=(target, level),
            device_id_type=MESH,
        )

    def send_label(offset, carry):
        label_copy(row_peer(me, offset), me).start()
        return carry

    def slots_of(stage, part):
        rows = pl.ds(part * CHUNK, CHUNK)
        if stage == 0:
            return kappa.at[rows, :]
        return (source if stage % 2 == 0 else fields).at[(stage - 1) // 2, rows, :]

    def spread_copy(stage, target, origin):
        return pltpu.make_async_remote_copy(
            src_ref=slots_of(stage, target),
            dst_ref=received[stage].at[pl.ds(origin * CHUNK, CHUNK), :],
            send_sem=spread_send.at[stage, target],
            recv_sem=spread_recv.at[stage, origin],
            device_id=(target, level),
            device_id_type=MESH,
        )

    def own_spread_copy(stage):
        return pltpu.make_async_copy(
            slots_of(stage, me),
            received[stage].at[pl.ds(me * CHUNK, CHUNK), :],
            own_spread.at[stage],
        )

    def spread(stage, first, last):
        def send_spread(turn, carry):
            spread_copy(stage, row_peer(me, (turn * 7) % WIDE), me).start()
            return carry

        lax.fori_loop(first, last, send_spread, 0)
        if first == 1:
            own_spread_copy(stage).start()

    def place_of(stage, origin):
        if stage == 0:
            return weight.at[pl.ds(origin * PIECE, PIECE), :]
        if stage % 2 == 0:
            return rhs[(stage - 1) // 2].at[pl.ds(origin * PIECE, PIECE), :]
        return cells[(stage - 1) // 2].at[pl.ds(origin * PIECE + PS, PIECE), :]

    def give_copy(stage, target, origin):
        return pltpu.make_async_remote_copy(
            src_ref=sending[stage].at[pl.ds(target * PIECE, PIECE), :],
            dst_ref=place_of(stage, origin),
            send_sem=give_send.at[stage, target],
            recv_sem=give_recv.at[stage, origin],
            device_id=(target, level),
            device_id_type=MESH,
        )

    def own_give_copy(stage):
        return pltpu.make_async_copy(
            sending[stage].at[pl.ds(me * PIECE, PIECE), :],
            place_of(stage, me),
            own_give.at[stage],
        )

    lane = lax.broadcasted_iota(jnp.int32, (8, LANES), 1)
    low_half = lane < 64
    low_quarter = lane % 64 < 32

    def give(stage):
        def wait_spread(turn, carry):
            origin = row_peer(me, turn)
            spread_copy(stage, origin, origin).wait_recv()
            return carry

        lax.fori_loop(1, WIDE, wait_spread, 0)
        own_spread_copy(stage).wait()

        def pick(owner, carry):
            starts = [start_smem[0, owner * 4 + part] for part in range(4)]
            v = [
                [
                    received[stage][pl.ds(start + plane * 64, 8, stride=8), :]
                    for start in starts
                ]
                for plane in range(2)
            ]
            for plane in range(2):
                a, b, c, d = v[plane]
                u = [
                    jnp.where(low_half, a, pltpu.roll(c, 64, 1)),
                    jnp.where(low_half, b, pltpu.roll(d, 64, 1)),
                    jnp.where(low_half, pltpu.roll(a, 64, 1), c),
                    jnp.where(low_half, pltpu.roll(b, 64, 1), d),
                ]
                w = [
                    jnp.where(low_quarter, u[0], pltpu.roll(u[1], 32, 1)),
                    jnp.where(low_quarter, pltpu.roll(u[0], 96, 1), u[1]),
                    jnp.where(low_quarter, u[2], pltpu.roll(u[3], 32, 1)),
                    jnp.where(low_quarter, pltpu.roll(u[2], 96, 1), u[3]),
                ]
                for part in range(4):
                    row = owner * PIECE + plane * PS + part
                    sending[stage][pl.ds(row, 8, stride=4), :] = w[part]
            return carry

        lax.fori_loop(0, WIDE, pick, 0)

        def send_give(turn, carry):
            give_copy(stage, row_peer(me, (turn * 7) % WIDE), me).start()
            return carry

        lax.fori_loop(1, WIDE, send_give, 0)
        own_give_copy(stage).start()

    def wait_given(stage):
        def wait_give(turn, carry):
            origin = row_peer(me, turn)
            give_copy(stage, origin, origin).wait_recv()
            return carry

        lax.fori_loop(1, WIDE, wait_give, 0)
        own_give_copy(stage).wait()

    ways = (
        (above, (me, level + 1), below),
        (below, (me, level - 1), above),
        (right, (me + 1, level), left),
        (left, (me - 1, level), right),
    )

    def face_copy(field, slot, way):
        return pltpu.make_async_remote_copy(
            src_ref=faces_out.at[field, slot, way],
            dst_ref=faces_in.at[field, slot, way],
            send_sem=face_send.at[field, slot, way],
            recv_sem=face_recv.at[field, slot, way],
            device_id=ways[way][1],
            device_id_type=MESH,
        )

    def face_sent(field, step):
        for way in range(4):

            @pl.when(ways[way][0])
            def _():
                face_copy(field, step % 2, way).wait_send()

    def post(field, step):
        slot = step % 2
        if step >= 2:
            face_sent(field, step - 2)
        block = cells[field]
        faces_out[field, slot, 0] = block[PS * PS : (PS + 1) * PS, :]
        faces_out[field, slot, 1] = block[PS : 2 * PS, :]
        for group in range(PS // 8):
            rows, row = pl.ds(group * 8, 8), (group * 8 + 1) * PS
            faces_out[field, slot, 2, rows, :] = block[pl.ds(row + PS - 1, 8, stride=PS), :]
            faces_out[field, slot, 3, rows, :] = block[pl.ds(row, 8, stride=PS), :]
        for way in (2, 3, 0, 1):

            @pl.when(ways[way][0])
            def _():
                face_copy(field, slot, way).start()

    row32 = lax.broadcasted_iota(jnp.int32, (PS, LANES), 0)
    lane32 = lax.broadcasted_iota(jnp.int32, (PS, LANES), 1)
    even = (row32 + lane32) % 2 == 0
    odd = (row32 + lane32) % 2 == 1
    first_row, last_row = row32 == 0, row32 == PS - 1
    first_lane, last_lane = lane32 == 0, lane32 == LANES - 1

    def relax(field, step):
        slot, colour = step % 2, step % 2
        for way in range(4):

            @pl.when(ways[way][2])
            def _():
                face_copy(field, slot, way).wait_recv()

        block, right_side = cells[field], rhs[field]
        block[0:PS, :] = faces_in[field, slot, 0]
        block[(PS + 1) * PS : (PS + 2) * PS, :] = faces_in[field, slot, 1]

        def several(group, carry):
            plane = group * GROUP
            v = [
                block[pl.ds(pl.multiple_of((plane + i) * PS, PS), PS), :]
                for i in range(GROUP + 2)
            ]
            fresh = []
            for i in range(GROUP):
                rows = pl.ds(pl.multiple_of((plane + i) * PS, PS), PS)
                mine = v[i + 1]
                low = jnp.broadcast_to(
                    faces_in[field, slot, 2, pl.ds(plane + i, 1), :], (PS, LANES)
                )
                high = jnp.broadcast_to(
                    faces_in[field, slot, 3, pl.ds(plane + i, 1), :], (PS, LANES)
                )
                total = v[i] + v[i + 2]
                total += jnp.where(first_row, low, pltpu.roll(mine, 1, 0))
                total += jnp.where(last_row, high, pltpu.roll(mine, PS - 1, 0))
                total += jnp.where(first_lane, 0.0, pltpu.roll(mine, 1, 1))
                total += jnp.where(last_lane, 0.0, pltpu.roll(mine, LANES - 1, 1))
                value = (right_side[rows, :] + total) * weight[rows, :] - 0.5 * mine
                fresh.append(jnp.where(even if i % 2 == colour else odd, value, mine))
            for i in range(GROUP):
                if step == HALF_SWEEPS - 1:
                    out[field, plane + i] = fresh[i]
                else:
                    rows = pl.ds(pl.multiple_of((plane + i + 1) * PS, PS), PS)
                    block[rows, :] = fresh[i]
            return carry

        lax.fori_loop(0, PS // GROUP, several, 0)

    lax.fori_loop(1, WIDE, send_label, 0)
    all_labels[pl.ds(me * SLOTS, SLOTS), :] = labels[...]
    for stage in range(4):
        spread(stage, 1, WIDE)

    def wait_label(offset, carry):
        origin = row_peer(me, offset)
        label_copy(origin, origin).wait_recv()
        return carry

    lax.fori_loop(1, WIDE, wait_label, 0)
    slot_row = lax.broadcasted_iota(jnp.int32, (WIDE * SLOTS, LANES), 0)
    wanted = lax.broadcasted_iota(jnp.int32, (WIDE * SLOTS, LANES), 1) + level * (WIDE * 4)
    first = (slot_row // SLOTS) * CHUNK + slot_row % SLOTS
    found = jnp.where(all_labels[...] == wanted, first, 0)
    start_vmem[...] = jnp.max(found, axis=0, keepdims=True)
    move = pltpu.make_async_copy(start_vmem, start_smem, start_sem)
    move.start()
    move.wait()

    half = WIDE // 2
    for stage in range(3):
        give(stage)
    spread(4, 1, half)
    wait_given(0)

    def invert(block, carry):
        rows = pl.ds(pl.multiple_of(block * PS, PS), PS)
        weight[rows, :] = 1.5 * (1.0 / (6.0 + weight[rows, :]))
        return carry

    lax.fori_loop(0, PS, invert, 0)
    wait_given(1)
    wait_given(2)

    between = {
        (0, 0): lambda: spread(4, half, WIDE),
        (0, 1): lambda: give(3),
        (0, 2): lambda: spread(5, 1, half),
        (0, 3): lambda: spread(5, half, WIDE),
        (0, 4): lambda: give(4),
        (0, 5): lambda: spread(6, 1, half),
        (1, 0): lambda: spread(6, half, WIDE),
        (1, 1): lambda: give(5),
        (1, 3): lambda: give(6),
    }
    for field in range(3):
        if field > 0:
            wait_given(2 * field + 1)
            wait_given(2 * field + 2)
        for step in range(HALF_SWEEPS):
            post(field, step)
            if (field, step) in between:
                between[field, step]()
            relax(field, step)

    for field in range(3):
        face_sent(field, HALF_SWEEPS - 2)
        face_sent(field, HALF_SWEEPS - 1)

    def drain(offset, carry):
        target = row_peer(me, offset)
        label_copy(target, me).wait_send()
        for stage in range(STAGES):
            spread_copy(stage, target, me).wait_send()
            give_copy(stage, target, me).wait_send()
        return carry

    lax.fori_loop(1, WIDE, drain, 0)


def local(old_fields, old_source, old_kappa, patch_ids):
    def tiles(array):
        lead = array.shape[:-2]
        split = array.reshape(lead + (SLOTS, -1, LANES))
        return jnp.swapaxes(split, -3, -2).reshape(lead + (-1, LANES))

    fields = tiles(jnp.swapaxes(old_fields, 0, 1))
    source = tiles(jnp.swapaxes(old_source, 0, 1))
    kappa = tiles(old_kappa)
    labels = jnp.broadcast_to(patch_ids[:, None], (SLOTS, LANES))
    vmem = pl.BlockSpec(memory_space=pltpu.VMEM)
    anywhere = pl.BlockSpec(memory_space=pl.ANY)
    dma = pltpu.SemaphoreType.DMA
    scratch = (
        [pltpu.VMEM((WIDE * CHUNK, LANES), F32)] * STAGES
        + [pltpu.VMEM((WIDE * PIECE, LANES), F32)] * STAGES
        + [pltpu.VMEM(((PS + 2) * PS, LANES), F32)] * 3
        + [pltpu.VMEM((PS * PS, LANES), F32)] * 3
        + [
            pltpu.VMEM((PS * PS, LANES), F32),
            pltpu.VMEM((WIDE * SLOTS, LANES), jnp.int32),
            pltpu.VMEM((1, LANES), jnp.int32),
            pltpu.SMEM((1, LANES), jnp.int32),
            pltpu.VMEM((3, 2, 4, PS, LANES), F32),
            pltpu.VMEM((3, 2, 4, PS, LANES), F32),
            dma((WIDE,)),
            dma((WIDE,)),
            dma((STAGES, WIDE)),
            dma((STAGES, WIDE)),
            dma((STAGES, WIDE)),
            dma((STAGES, WIDE)),
            dma((STAGES,)),
            dma((STAGES,)),
            dma(()),
            dma((3, 2, 4)),
            dma((3, 2, 4)),
        ]
    )
    return pl.pallas_call(
        kernel,
        out_shape=jax.ShapeDtypeStruct((3, PS, PS, LANES), F32),
        in_specs=[anywhere, anywhere, anywhere, vmem],
        out_specs=vmem,
        scratch_shapes=scratch,
        compiler_params=pltpu.CompilerParams(
            collective_id=0, has_side_effects=True, vmem_limit_bytes=60 << 20
        ),
        name="regrid_and_sweep",
    )(fields, source, kappa, labels)


def solution(mesh):
    in_specs = (
        P(("wide", "narrow"), None, None),
        P(("wide", "narrow"), None, None),
        P(("wide", "narrow"), None),
        P(("wide", "narrow")),
    )
    out_specs = P(None, "narrow", "wide", None)
    return jax.shard_map(local, mesh=mesh, in_specs=in_specs, out_specs=out_specs, check_vma=False)
```

time: 185 us -> 184 us (level)
  Pallas kernels: 181 us -> 179 us
where the time goes in v2:
time: 184 us; the launch traced here: 183 us
  Pallas kernels  179 us (97%)
  local copies, waits for them, and re-layouts  3.98 us (2%)
    pallas_call x1, Pallas kernels, local(): pl.pallas_call(kernel, out_shape=jax.ShapeDtypeStruct((3, PS, PS, LANES),...  179 us

profile of v2, /device:TPU:40, one launch (start us, length us, event | category | flops | bytes accessed | tf_op | source)
XLA Modules:
  0.0 183.3 jit_solution(15507800842898697236)
XLA Ops:
  0.0 1.3 broadcast_in_dim.2.labels
  1.3 179.3 %regrid_and_sweep.1 = f32[3,32,32,128]{3,2,1,0:T(8,128)} custom-call(f32[3,2048,128]{2,1,0:T(8,128)} %bitcast.19, f32[3,2048,128]{2,1,0:T(8,128)} %bitcast.20, f32[2048,128]{1,0:T(8,128)} %bitcast.21, s32[8,128]{1,0:T(8,128)} %broadcast_in_dim.2.labels), custom_call_target="tpu_custom_call" | custom-call | tf_op jit(solution)/shard_map/regrid_and_sweep/pallas_call | solution.py:398
  180.6 2.7 %copy.6 = f32[3,32,32,128]{3,2,1,0:T(8,128)} copy(f32[3,32,32,128]{3,2,1,0:T(8,128)} %regrid_and_sweep.1) | data formatting | bytes 3145728

commit v3 on v2

--- a/solution.py
+++ b/solution.py
@@ -288,7 +288,7 @@
 
     lax.fori_loop(1, WIDE, send_label, 0)
     all_labels[pl.ds(me * SLOTS, SLOTS), :] = labels[...]
-    for stage in range(4):
+    for stage in range(STAGES):
         spread(stage, 1, WIDE)
 
     def wait_label(offset, carry):
@@ -306,10 +306,8 @@
     move.start()
     move.wait()
 
-    half = WIDE // 2
-    for stage in range(3):
+    for stage in range(STAGES):
         give(stage)
-    spread(4, 1, half)
     wait_given(0)
 
     def invert(block, carry):
@@ -318,29 +316,16 @@
         return carry
 
     lax.fori_loop(0, PS, invert, 0)
-    wait_given(1)
-    wait_given(2)
-
-    between = {
-        (0, 0): lambda: spread(4, half, WIDE),
-        (0, 1): lambda: give(3),
-        (0, 2): lambda: spread(5, 1, half),
-        (0, 3): lambda: spread(5, half, WIDE),
-        (0, 4): lambda: give(4),
-        (0, 5): lambda: spread(6, 1, half),
-        (1, 0): lambda: spread(6, half, WIDE),
-        (1, 1): lambda: give(5),
-        (1, 3): lambda: give(6),
-    }
     for field in range(3):
-        if field > 0:
-            wait_given(2 * field + 1)
-            wait_given(2 * field + 2)
-        for step in range(HALF_SWEEPS):
-            post(field, step)
-            if (field, step) in between:
-                between[field, step]()
+        wait_given(2 * field + 1)
+        wait_given(2 * field + 2)
+        post(field, 0)
+
+    for step in range(HALF_SWEEPS):
+        for field in range(3):
             relax(field, step)
+            if step < HALF_SWEEPS - 1:
+                post(field, step + 1)
 
     for field in range(3):
         face_sent(field, HALF_SWEEPS - 2)

time: 184 us -> 167 us (0.908)
  Pallas kernels: 179 us -> 162 us
    pallas_call x1, Pallas kernels: 179 us -> 162 us  [local(): pl.pallas_call(kernel, out_shape=jax.ShapeDtypeStruct((3, PS, PS, LANES),...]
where the time goes in v3:
time: 167 us; the launch traced here: 166 us
  Pallas kernels  162 us (97%)
  local copies, waits for them, and re-layouts  3.98 us (2%)
    pallas_call x1, Pallas kernels, local(): pl.pallas_call(kernel, out_shape=jax.ShapeDtypeStruct((3, PS, PS, LANES),...  162 us

profile of v3, /device:TPU:40, one launch (start us, length us, event | category | flops | bytes accessed | tf_op | source)
XLA Modules:
  0.0 166.1 jit_solution(15178667525090015837)
XLA Ops:
  0.0 1.3 broadcast_in_dim.2.labels
  1.3 162.1 %regrid_and_sweep.1 = f32[3,32,32,128]{3,2,1,0:T(8,128)} custom-call(f32[3,2048,128]{2,1,0:T(8,128)} %bitcast.19, f32[3,2048,128]{2,1,0:T(8,128)} %bitcast.20, f32[2048,128]{1,0:T(8,128)} %bitcast.21, s32[8,128]{1,0:T(8,128)} %broadcast_in_dim.2.labels), custom_call_target="tpu_custom_call" | custom-call | tf_op jit(solution)/shard_map/regrid_and_sweep/pallas_call | solution.py:383
  163.4 2.7 %copy.6 = f32[3,32,32,128]{3,2,1,0:T(8,128)} copy(f32[3,32,32,128]{3,2,1,0:T(8,128)} %regrid_and_sweep.1) | data formatting | bytes 3145728

commit v4 on v3

v4 whole, which is shorter than its diff:
```python
import jax
import jax.numpy as jnp
from jax import lax
from jax.experimental import pallas as pl
from jax.experimental.pallas import tpu as pltpu
from jax.sharding import PartitionSpec as P

PS = 32
SLOTS = 8
LANES = 128
WIDE = 16
STAGES = 7
PLANE = 64
ZONE_IN, DEEP_IN = 96, 32
ZONE_OUT, DEEP_OUT = 48, 16
HALF_SWEEPS = 6
GROUP = 4
MESH = pl.DeviceIdType.MESH
F32 = jnp.float32


def row_peer(me, offset):
    row = lax.rem(me // 4 + offset // 4, 4)
    column = lax.rem(lax.rem(me, 4) + lax.rem(offset, 4), 4)
    return row * 4 + column


def kernel(fields, source, kappa, labels, out, *scratch):
    received, sending, landed = (
        [scratch[group * STAGES : (group + 1) * STAGES] for group in (first, first + 1)]
        for first in (0, 2, 4)
    )
    cells = scratch[6 * STAGES : 6 * STAGES + 3]
    rhs = scratch[6 * STAGES + 3 : 6 * STAGES + 6]
    (
        weight, all_labels, start_vmem, start_smem, faces_out, faces_in,
        label_send, label_recv, spread_send, spread_recv, give_send, give_recv,
        own_spread, own_give, start_sem, face_send, face_recv,
    ) = scratch[6 * STAGES + 6 :]
    me = lax.axis_index("wide")
    level = lax.axis_index("narrow")
    levels = lax.axis_size("narrow")
    below, above = level > 0, level < levels - 1
    left, right = me > 0, me < WIDE - 1

    faces_in[...] = jnp.zeros_like(faces_in)

    barrier = pltpu.get_barrier_semaphore()

    def greet(offset, carry):
        pl.semaphore_signal(
            barrier, inc=1, device_id=(row_peer(me, offset), level), device_id_type=MESH
        )
        return carry

    lax.fori_loop(1, WIDE, greet, 0)

    @pl.when(below)
    def _():
        pl.semaphore_signal(barrier, inc=1, device_id=(me, level - 1), device_id_type=MESH)

    @pl.when(above)
    def _():
        pl.semaphore_signal(barrier, inc=1, device_id=(me, level + 1), device_id_type=MESH)

    pl.semaphore_wait(
        barrier, WIDE - 1 + below.astype(jnp.int32) + above.astype(jnp.int32)
    )

    def label_copy(target, origin):
        return pltpu.make_async_remote_copy(
            src_ref=labels,
            dst_ref=all_labels.at[pl.ds(origin * SLOTS, SLOTS), :],
            send_sem=label_send.at[target],
            recv_sem=label_recv.at[origin],
            device_id=(target, level),
            device_id_type=MESH,
        )

    def send_label(offset, carry):
        label_copy(row_peer(me, offset), me).start()
        return carry

    def outer_plane(part):
        return part + part // 8 * 16

    def pieces(deep):
        return (3,) if deep else (0, 1, 2)

    def slots_of(stage, part, piece):
        inner = (part + 8) * PLANE
        first, count = (
            (outer_plane(part) * PLANE, PLANE), (inner, 16), (inner + 48, 16), (inner + 16, 32),
        )[piece]
        rows = pl.ds(first, count)
        if stage == 0:
            return kappa.at[rows, :]
        return (source if stage % 2 == 0 else fields).at[(stage - 1) // 2, rows, :]

    def slots_at(stage, origin, piece):
        if piece == 3:
            return received[1][stage].at[pl.ds(origin * DEEP_IN, DEEP_IN), :]
        first, count = ((0, PLANE), (PLANE, 16), (PLANE + 16, 16))[piece]
        return received[0][stage].at[pl.ds(origin * ZONE_IN + first, count), :]

    def spread_copy(stage, target, origin, piece):
        return pltpu.make_async_remote_copy(
            src_ref=slots_of(stage, target, piece),
            dst_ref=slots_at(stage, origin, piece),
            send_sem=spread_send.at[stage * 4 + piece, target],
            recv_sem=spread_recv.at[stage * 4 + piece, origin],
            device_id=(target, level),
            device_id_type=MESH,
        )

    def own_spread_copy(stage, piece):
        return pltpu.make_async_copy(
            slots_of(stage, me, piece),
            slots_at(stage, me, piece),
            own_spread.at[stage * 4 + piece],
        )

    def spread(stage, deep):
        def send_spread(turn, carry):
            for piece in pieces(deep):
                spread_copy(stage, row_peer(me, (turn * 7) % WIDE), me, piece).start()
            return carry

        lax.fori_loop(1, WIDE, send_spread, 0)
        for piece in pieces(deep):
            own_spread_copy(stage, piece).start()

    def give_copy(stage, target, origin, deep):
        rows = DEEP_OUT if deep else ZONE_OUT
        return pltpu.make_async_remote_copy(
            src_ref=sending[deep][stage].at[pl.ds(target * rows, rows), :],
            dst_ref=landed[deep][stage].at[pl.ds(origin * rows, rows), :],
            send_sem=give_send.at[stage * 2 + deep, target],
            recv_sem=give_recv.at[stage * 2 + deep, origin],
            device_id=(target, level),
            device_id_type=MESH,
        )

    def own_give_copy(stage, deep):
        rows = pl.ds(me * (DEEP_OUT if deep else ZONE_OUT), DEEP_OUT if deep else ZONE_OUT)
        return pltpu.make_async_copy(
            sending[deep][stage].at[rows, :],
            landed[deep][stage].at[rows, :],
            own_give.at[stage * 2 + deep],
        )

    def turn_over(patches, lines):
        lane = lax.broadcasted_iota(jnp.int32, (lines, LANES), 1)
        low_half = lane < 64
        low_quarter = lane % 64 < 32
        a, b, c, d = patches
        u = [
            jnp.where(low_half, a, pltpu.roll(c, 64, 1)),
            jnp.where(low_half, b, pltpu.roll(d, 64, 1)),
            jnp.where(low_half, pltpu.roll(a, 64, 1), c),
            jnp.where(low_half, pltpu.roll(b, 64, 1), d),
        ]
        return [
            jnp.where(low_quarter, u[0], pltpu.roll(u[1], 32, 1)),
            jnp.where(low_quarter, pltpu.roll(u[0], 96, 1), u[1]),
            jnp.where(low_quarter, u[2], pltpu.roll(u[3], 32, 1)),
            jnp.where(low_quarter, pltpu.roll(u[2], 96, 1), u[3]),
        ]

    def give(stage, deep):
        def wait_spread(turn, carry):
            origin = row_peer(me, turn)
            for piece in pieces(deep):
                spread_copy(stage, origin, origin, piece).wait_recv()
            return carry

        lax.fori_loop(1, WIDE, wait_spread, 0)
        for piece in pieces(deep):
            own_spread_copy(stage, piece).wait()
        source_rows, finished = received[deep][stage], sending[deep][stage]
        runs = ((0, 4, 0),) if deep else ((0, 8, 0), (PLANE, 4, 32))

        def pick(owner, carry):
            starts = [start_smem[deep, owner * 4 + part] for part in range(4)]
            taken = [
                [source_rows[pl.ds(start + first, lines, stride=8), :] for start in starts]
                for first, lines, _ in runs
            ]
            for (_, lines, row), patches in zip(runs, taken):
                base = owner * (DEEP_OUT if deep else ZONE_OUT) + row
                for part, value in enumerate(turn_over(patches, lines)):
                    finished[pl.ds(base + part, lines, stride=4), :] = value
            return carry

        lax.fori_loop(0, WIDE, pick, 0)

        def send_give(turn, carry):
            give_copy(stage, row_peer(me, (turn * 7) % WIDE), me, deep).start()
            return carry

        lax.fori_loop(1, WIDE, send_give, 0)
        own_give_copy(stage, deep).start()

    def settle(stage, deep):
        def wait_give(turn, carry):
            origin = row_peer(me, turn)
            give_copy(stage, origin, origin, deep).wait_recv()
            return carry

        lax.fori_loop(1, WIDE, wait_give, 0)
        own_give_copy(stage, deep).wait()
        shift = 0
        if stage == 0:
            home = weight
        elif stage % 2 == 0:
            home = rhs[(stage - 1) // 2]
        else:
            home, shift = cells[(stage - 1) // 2], 1
        here = landed[deep][stage]

        def put(part, carry):
            outer = (outer_plane(part) + shift) * PS
            inner = (part + 8 + shift) * PS
            moves = (
                ((0, inner + 8, 16),)
                if deep
                else ((0, outer, 32), (32, inner, 8), (40, inner + 24, 8))
            )
            for first, row, count in moves:
                first += part * (DEEP_OUT if deep else ZONE_OUT)
                value = here[pl.ds(pl.multiple_of(first, 8), count), :]
                if stage == 0:
                    value = 1.5 * (1.0 / (6.0 + value))
                home[pl.ds(pl.multiple_of(row, 8), count), :] = value
            return carry

        lax.fori_loop(0, WIDE, put, 0)

    ways = (
        (above, (me, level + 1), below),
        (below, (me, level - 1), above),
        (right, (me + 1, level), left),
        (left, (me - 1, level), right),
    )

    def face_copy(field, slot, way):
        return pltpu.make_async_remote_copy(
            src_ref=faces_out.at[field, slot, way],
            dst_ref=faces_in.at[field, slot, way],
            send_sem=face_send.at[field, slot, way],
            recv_sem=face_recv.at[field, slot, way],
            device_id=ways[way][1],
            device_id_type=MESH,
        )

    def face_sent(field, step):
        for way in range(4):

            @pl.when(ways[way][0])
            def _():
                face_copy(field, step % 2, way).wait_send()

    def post(field, step):
        slot = step % 2
        if step >= 2:
            face_sent(field, step - 2)
        block = cells[field]
        faces_out[field, slot, 0] = block[PS * PS : (PS + 1) * PS, :]
        faces_out[field, slot, 1] = block[PS : 2 * PS, :]
        for group in range(PS // 8):
            rows, row = pl.ds(group * 8, 8), (group * 8 + 1) * PS
            faces_out[field, slot, 2, rows, :] = block[pl.ds(row + PS - 1, 8, stride=PS), :]
            faces_out[field, slot, 3, rows, :] = block[pl.ds(row, 8, stride=PS), :]
        for way in (2, 3, 0, 1):

            @pl.when(ways[way][0])
            def _():
                face_copy(field, slot, way).start()

    def new_values(v, low, high, right_side, w, chosen):
        rows = v[0].shape[0]
        row = lax.broadcasted_iota(jnp.int32, (rows, LANES), 0)
        lane = lax.broadcasted_iota(jnp.int32, (rows, LANES), 1)
        fresh = []
        for i in range(len(v) - 2):
            mine = v[i + 1]
            back, forth = pltpu.roll(mine, 1, 0), pltpu.roll(mine, rows - 1, 0)
            if low is not None:
                back = jnp.where(row == 0, jnp.broadcast_to(low[i], mine.shape), back)
            if high is not None:
                forth = jnp.where(row == rows - 1, jnp.broadcast_to(high[i], mine.shape), forth)
            total = v[i] + v[i + 2] + back + forth
            total += jnp.where(lane == 0, 0.0, pltpu.roll(mine, 1, 1))
            total += jnp.where(lane == LANES - 1, 0.0, pltpu.roll(mine, LANES - 1, 1))
            value = (right_side[i] + total) * w[i] - 0.5 * mine
            fresh.append(jnp.where(chosen[i], value, mine))
        return fresh

    row32 = lax.broadcasted_iota(jnp.int32, (PS, LANES), 0)
    lane32 = lax.broadcasted_iota(jnp.int32, (PS, LANES), 1)
    row_reach = jnp.abs(2 * row32 - (PS - 1))
    even = (row32 + lane32) % 2 == 0
    odd = (row32 + lane32) % 2 == 1

    def relax_outside(field, step):
        slot, colour = step % 2, step % 2
        for way in range(4):

            @pl.when(ways[way][2])
            def _():
                face_copy(field, slot, way).wait_recv()

        block, right_side = cells[field], rhs[field]
        block[0:PS, :] = faces_in[field, slot, 0]
        block[(PS + 1) * PS : (PS + 2) * PS, :] = faces_in[field, slot, 1]

        def part_of(array, plane, first, count):
            return array[pl.ds(pl.multiple_of(plane * PS + first, 8), count), :]

        def several(group, carry):
            plane = group * GROUP + group // 2 * 16
            fresh = new_values(
                [part_of(block, plane + i, 0, PS) for i in range(GROUP + 2)],
                [faces_in[field, slot, 2, pl.ds(plane + i, 1), :] for i in range(GROUP)],
                [faces_in[field, slot, 3, pl.ds(plane + i, 1), :] for i in range(GROUP)],
                [part_of(right_side, plane + i, 0, PS) for i in range(GROUP)],
                [part_of(weight, plane + i, 0, PS) for i in range(GROUP)],
                [
                    (even if i % 2 == colour else odd)
                    & (
                        jnp.maximum(row_reach, jnp.abs(2 * (plane + i) - (PS - 1)))
                        >= 19 + 2 * step
                    )
                    for i in range(GROUP)
                ],
            )
            for i in range(GROUP):
                rows = pl.ds(pl.multiple_of((plane + i + 1) * PS, PS), PS)
                block[rows, :] = fresh[i]
            return carry

        lax.fori_loop(0, 4, several, 0)
        row8 = lax.broadcasted_iota(jnp.int32, (8, LANES), 0)
        lane8 = lax.broadcasted_iota(jnp.int32, (8, LANES), 1)
        reach = (row8 <= 6 - step, row8 >= 1 + step)

        def ends(group, carry):
            plane = group * GROUP + 8
            fresh = []
            for end, first in ((0, 0), (1, 24)):
                line = [
                    faces_in[field, slot, 2 + end, pl.ds(plane + i, 1), :] for i in range(GROUP)
                ]
                fresh.append(
                    new_values(
                        [part_of(block, plane + i, first, 8) for i in range(GROUP + 2)],
                        line if end == 0 else None,
                        line if end == 1 else None,
                        [part_of(right_side, plane + i, first, 8) for i in range(GROUP)],
                        [part_of(weight, plane + i, first, 8) for i in range(GROUP)],
                        [
                            ((row8 + lane8 + i) % 2 == colour) & reach[end]
                            for i in range(GROUP)
                        ],
                    )
                )
            for end, first in ((0, 0), (1, 24)):
                for i in range(GROUP):
                    row = (plane + i + 1) * PS + first
                    block[pl.ds(pl.multiple_of(row, 8), 8), :] = fresh[end][i]
            return carry

        lax.fori_loop(0, 4, ends, 0)

    def relax_inside(field, step):
        colour = step % 2
        block, right_side = cells[field], rhs[field]
        start, groups = ((6, 5), (6, 5), (4, 6), (4, 6), (2, 7), (0, 8))[step]

        def several(group, carry):
            plane = group * GROUP + start

            def whole(array, i):
                return array[pl.ds(pl.multiple_of((plane + i) * PS, PS), PS), :]

            fresh = new_values(
                [whole(block, i) for i in range(GROUP + 2)],
                None,
                None,
                [whole(right_side, i) for i in range(GROUP)],
                [whole(weight, i) for i in range(GROUP)],
                [
                    (even if i % 2 == colour else odd)
                    & (
                        jnp.maximum(row_reach, jnp.abs(2 * (plane + i) - (PS - 1)))
                        < 19 + 2 * step
                    )
                    for i in range(GROUP)
                ],
            )
            for i in range(GROUP):
                if step == HALF_SWEEPS - 1:
                    out[field, plane + i] = fresh[i]
                else:
                    rows = pl.ds(pl.multiple_of((plane + i + 1) * PS, PS), PS)
                    block[rows, :] = fresh[i]
            return carry

        lax.fori_loop(0, groups, several, 0)

    lax.fori_loop(1, WIDE, send_label, 0)
    all_labels[pl.ds(me * SLOTS, SLOTS), :] = labels[...]
    for stage in range(STAGES):
        spread(stage, 0)

    def wait_label(offset, carry):
        origin = row_peer(me, offset)
        label_copy(origin, origin).wait_recv()
        return carry

    lax.fori_loop(1, WIDE, wait_label, 0)
    slot_row = lax.broadcasted_iota(jnp.int32, (WIDE * SLOTS, LANES), 0)
    wanted = lax.broadcasted_iota(jnp.int32, (WIDE * SLOTS, LANES), 1) + level * (WIDE * 4)
    for deep, rows in ((0, ZONE_IN), (1, DEEP_IN)):
        first = (slot_row // SLOTS) * rows + slot_row % SLOTS
        found = jnp.where(all_labels[...] == wanted, first, 0)
        start_vmem[deep : deep + 1, :] = jnp.max(found, axis=0, keepdims=True)
    move = pltpu.make_async_copy(start_vmem, start_smem, start_sem)
    move.start()
    move.wait()

    for stage in range(STAGES):
        give(stage, 0)
    for stage in range(2):
        spread(stage, 1)
    settle(0, 0)
    for field in range(3):
        settle(2 * field + 1, 0)
        settle(2 * field + 2, 0)
        post(field, 0)

    between = (
        ((spread, 2), (spread, 3)),
        ((give, 0), (spread, 4)),
        ((give, 1), (give, 2), (spread, 5)),
        ((give, 3), (spread, 6)),
        ((give, 4), (give, 5)),
        ((give, 6),),
    )
    for step in range(HALF_SWEEPS):
        for move_on, stage in between[step]:
            move_on(stage, 1)
        for field in range(3):
            relax_outside(field, step)
            if step < HALF_SWEEPS - 1:
                post(field, step + 1)
    settle(0, 1)
    for field in range(3):
        settle(2 * field + 1, 1)
        settle(2 * field + 2, 1)
        for step in range(HALF_SWEEPS):
            relax_inside(field, step)

    for field in range(3):
        face_sent(field, HALF_SWEEPS - 2)
        face_sent(field, HALF_SWEEPS - 1)

    def drain(offset, carry):
        target = row_peer(me, offset)
        label_copy(target, me).wait_send()
        for stage in range(STAGES):
            for piece in range(4):
                spread_copy(stage, target, me, piece).wait_send()
            for deep in range(2):
                give_copy(stage, target, me, deep).wait_send()
        return carry

    lax.fori_loop(1, WIDE, drain, 0)


def local(old_fields, old_source, old_kappa, patch_ids):
    def tiles(array):
        lead = array.shape[:-2]
        split = array.reshape(lead + (SLOTS, -1, LANES))
        return jnp.swapaxes(split, -3, -2).reshape(lead + (-1, LANES))

    fields = tiles(jnp.swapaxes(old_fields, 0, 1))
    source = tiles(jnp.swapaxes(old_source, 0, 1))
    kappa = tiles(old_kappa)
    labels = jnp.broadcast_to(patch_ids[:, None], (SLOTS, LANES))
    vmem = pl.BlockSpec(memory_space=pltpu.VMEM)
    anywhere = pl.BlockSpec(memory_space=pl.ANY)
    dma = pltpu.SemaphoreType.DMA
    scratch = (
        [
            pltpu.VMEM((WIDE * rows, LANES), F32)
            for rows in (ZONE_IN, DEEP_IN, ZONE_OUT, DEEP_OUT, ZONE_OUT, DEEP_OUT)
            for _ in range(STAGES)
        ]
        + [pltpu.VMEM(((PS + 2) * PS, LANES), F32)] * 3
        + [pltpu.VMEM((PS * PS, LANES), F32)] * 3
        + [
            pltpu.VMEM((PS * PS, LANES), F32),
            pltpu.VMEM((WIDE * SLOTS, LANES), jnp.int32),
            pltpu.VMEM((2, LANES), jnp.int32),
            pltpu.SMEM((2, LANES), jnp.int32),
            pltpu.VMEM((3, 2, 4, PS, LANES), F32),
            pltpu.VMEM((3, 2, 4, PS, LANES), F32),
            dma((WIDE,)),
            dma((WIDE,)),
            dma((STAGES * 4, WIDE)),
            dma((STAGES * 4, WIDE)),
            dma((STAGES * 2, WIDE)),
            dma((STAGES * 2, WIDE)),
            dma((STAGES * 4,)),
            dma((STAGES * 2,)),
            dma(()),
            dma((3, 2, 4)),
            dma((3, 2, 4)),
        ]
    )
    return pl.pallas_call(
        kernel,
        out_shape=jax.ShapeDtypeStruct((3, PS, PS, LANES), F32),
        in_specs=[anywhere, anywhere, anywhere, vmem],
        out_specs=vmem,
        scratch_shapes=scratch,
        compiler_params=pltpu.CompilerParams(
            collective_id=0, has_side_effects=True, vmem_limit_bytes=60 << 20
        ),
        name="regrid_and_sweep",
    )(fields, source, kappa, labels)


def solution(mesh):
    in_specs = (
        P(("wide", "narrow"), None, None),
        P(("wide", "narrow"), None, None),
        P(("wide", "narrow"), None),
        P(("wide", "narrow")),
    )
    out_specs = P(None, "narrow", "wide", None)
    return jax.shard_map(local, mesh=mesh, in_specs=in_specs, out_specs=out_specs, check_vma=False)
```

time: 167 us -> 177 us (1.060)
  Pallas kernels: 162 us -> 172 us
    pallas_call x1, Pallas kernels: 162 us -> 172 us  [local(): pl.pallas_call(kernel, out_shape=jax.ShapeDtypeStruct((3, PS, PS, LANES),...]
where the time goes in v4:
time: 177 us; the launch traced here: 176 us
  Pallas kernels  172 us (97%)
  local copies, waits for them, and re-layouts  3.98 us (2%)
    pallas_call x1, Pallas kernels, local(): pl.pallas_call(kernel, out_shape=jax.ShapeDtypeStruct((3, PS, PS, LANES),...  172 us

profile of v4, /device:TPU:40, one launch (start us, length us, event | category | flops | bytes accessed | tf_op | source)
XLA Modules:
  0.0 176.5 jit_solution(11251442767939964173)
XLA Ops:
  0.0 1.3 broadcast_in_dim.2.labels
  1.3 172.5 %regrid_and_sweep.1 = f32[3,32,32,128]{3,2,1,0:T(8,128)} custom-call(f32[3,2048,128]{2,1,0:T(8,128)} %bitcast.19, f32[3,2048,128]{2,1,0:T(8,128)} %bitcast.20, f32[2048,128]{1,0:T(8,128)} %bitcast.21, s32[8,128]{1,0:T(8,128)} %broadcast_in_dim.2.labels), custom_call_target="tpu_custom_call" | custom-call | tf_op jit(solution)/shard_map/regrid_and_sweep/pallas_call | solution.py:522
  173.8 2.7 %copy.6 = f32[3,32,32,128]{3,2,1,0:T(8,128)} copy(f32[3,32,32,128]{3,2,1,0:T(8,128)} %regrid_and_sweep.1) | data formatting | bytes 3145728

commit v5 on v3

--- a/solution.py
+++ b/solution.py
@@ -10,6 +10,7 @@
 LANES = 128
 WIDE = 16
 STAGES = 7
+FIELD, SIDE = 1, 4
 CHUNK = 128
 PIECE = 64
 HALF_SWEEPS = 6
@@ -24,13 +25,13 @@
     return row * 4 + column
 
 
-def kernel(fields, source, kappa, labels, out, *scratch):
+def kernel(fields, source, kappa, ids, out, *scratch):
     received = scratch[0:STAGES]
     sending = scratch[STAGES : 2 * STAGES]
     cells = scratch[2 * STAGES : 2 * STAGES + 3]
     rhs = scratch[2 * STAGES + 3 : 2 * STAGES + 6]
     (
-        weight, all_labels, start_vmem, start_smem, faces_out, faces_in,
+        labels, weight, lines, all_labels, start_vmem, start_smem, faces_out, faces_in,
         label_send, label_recv, spread_send, spread_recv, give_send, give_recv,
         own_spread, own_give, start_sem, face_send, face_recv,
     ) = scratch[2 * STAGES + 6 :]
@@ -40,6 +41,12 @@
     below, above = level > 0, level < levels - 1
     left, right = me > 0, me < WIDE - 1
 
+    tile_row = lax.broadcasted_iota(jnp.int32, (SLOTS, LANES), 0)
+    tile = jnp.zeros((SLOTS, LANES), jnp.int32)
+    for entry in range(SLOTS):
+        tile = jnp.where(tile_row == entry, ids[entry], tile)
+    labels[...] = tile
+
     faces_in[...] = jnp.zeros_like(faces_in)
 
     barrier = pltpu.get_barrier_semaphore()
@@ -82,7 +89,9 @@
         rows = pl.ds(part * CHUNK, CHUNK)
         if stage == 0:
             return kappa.at[rows, :]
-        return (source if stage % 2 == 0 else fields).at[(stage - 1) // 2, rows, :]
+        if stage < SIDE:
+            return fields.at[stage - FIELD, rows, :]
+        return source.at[stage - SIDE, rows, :]
 
     def spread_copy(stage, target, origin):
         return pltpu.make_async_remote_copy(
@@ -113,9 +122,9 @@
     def place_of(stage, origin):
         if stage == 0:
             return weight.at[pl.ds(origin * PIECE, PIECE), :]
-        if stage % 2 == 0:
-            return rhs[(stage - 1) // 2].at[pl.ds(origin * PIECE, PIECE), :]
-        return cells[(stage - 1) // 2].at[pl.ds(origin * PIECE + PS, PIECE), :]
+        if stage < SIDE:
+            return cells[stage - FIELD].at[pl.ds(origin * PIECE + PS, PIECE), :]
+        return rhs[stage - SIDE].at[pl.ds(origin * PIECE, PIECE), :]
 
     def give_copy(stage, target, origin):
         return pltpu.make_async_remote_copy(
@@ -217,17 +226,24 @@
             def _():
                 face_copy(field, step % 2, way).wait_send()
 
+    row8 = lax.broadcasted_iota(jnp.int32, (8, LANES), 0)
+    lane8 = lax.broadcasted_iota(jnp.int32, (8, LANES), 1)
+
     def post(field, step):
         slot = step % 2
         if step >= 2:
             face_sent(field, step - 2)
         block = cells[field]
-        faces_out[field, slot, 0] = block[PS * PS : (PS + 1) * PS, :]
-        faces_out[field, slot, 1] = block[PS : 2 * PS, :]
-        for group in range(PS // 8):
-            rows, row = pl.ds(group * 8, 8), (group * 8 + 1) * PS
-            faces_out[field, slot, 2, rows, :] = block[pl.ds(row + PS - 1, 8, stride=PS), :]
-            faces_out[field, slot, 3, rows, :] = block[pl.ds(row, 8, stride=PS), :]
+        for way, near in ((2, PS - 1), (3, 0), (0, PS - 1), (1, 0)):
+            if way < 2:
+                start = (near + 1) * PS
+                face = [block[start + 8 * i : start + 8 * i + 8, :] for i in range(4)]
+            else:
+                face = [block[pl.ds((8 * i + 1) * PS + near, 8, stride=PS), :] for i in range(4)]
+            kept = (row8 + lane8) % 2 == (1 - step % 2 + near) % 2
+            for i in range(2):
+                mixed = jnp.where(kept, face[i], pltpu.roll(face[i + 2], 1, 1))
+                faces_out[field, slot, way, 8 * i : 8 * i + 8, :] = mixed
         for way in (2, 3, 0, 1):
 
             @pl.when(ways[way][0])
@@ -250,8 +266,11 @@
                 face_copy(field, slot, way).wait_recv()
 
         block, right_side = cells[field], rhs[field]
-        block[0:PS, :] = faces_in[field, slot, 0]
-        block[(PS + 1) * PS : (PS + 2) * PS, :] = faces_in[field, slot, 1]
+        for way in range(4):
+            home, start = ((block, 0), (block, (PS + 1) * PS), (lines.at[field, 0], 0), (lines.at[field, 1], 0))[way]
+            mixed = faces_in[field, slot, way]
+            home[start : start + PS // 2, :] = mixed
+            home[start + PS // 2 : start + PS, :] = pltpu.roll(mixed, LANES - 1, 1)
 
         def several(group, carry):
             plane = group * GROUP
@@ -264,10 +283,10 @@
                 rows = pl.ds(pl.multiple_of((plane + i) * PS, PS), PS)
                 mine = v[i + 1]
                 low = jnp.broadcast_to(
-                    faces_in[field, slot, 2, pl.ds(plane + i, 1), :], (PS, LANES)
+                    lines[field, 0, pl.ds(plane + i, 1), :], (PS, LANES)
                 )
                 high = jnp.broadcast_to(
-                    faces_in[field, slot, 3, pl.ds(plane + i, 1), :], (PS, LANES)
+                    lines[field, 1, pl.ds(plane + i, 1), :], (PS, LANES)
                 )
                 total = v[i] + v[i + 2]
                 total += jnp.where(first_row, low, pltpu.roll(mine, 1, 0))
@@ -317,12 +336,13 @@
 
     lax.fori_loop(0, PS, invert, 0)
     for field in range(3):
-        wait_given(2 * field + 1)
-        wait_given(2 * field + 2)
+        wait_given(FIELD + field)
         post(field, 0)
 
     for step in range(HALF_SWEEPS):
         for field in range(3):
+            if step == 0:
+                wait_given(SIDE + field)
             relax(field, step)
             if step < HALF_SWEEPS - 1:
                 post(field, step + 1)
@@ -351,7 +371,6 @@
     fields = tiles(jnp.swapaxes(old_fields, 0, 1))
     source = tiles(jnp.swapaxes(old_source, 0, 1))
     kappa = tiles(old_kappa)
-    labels = jnp.broadcast_to(patch_ids[:, None], (SLOTS, LANES))
     vmem = pl.BlockSpec(memory_space=pltpu.VMEM)
     anywhere = pl.BlockSpec(memory_space=pl.ANY)
     dma = pltpu.SemaphoreType.DMA
@@ -361,12 +380,14 @@
         + [pltpu.VMEM(((PS + 2) * PS, LANES), F32)] * 3
         + [pltpu.VMEM((PS * PS, LANES), F32)] * 3
         + [
+            pltpu.VMEM((SLOTS, LANES), jnp.int32),
             pltpu.VMEM((PS * PS, LANES), F32),
+            pltpu.VMEM((3, 2, PS, LANES), F32),
             pltpu.VMEM((WIDE * SLOTS, LANES), jnp.int32),
             pltpu.VMEM((1, LANES), jnp.int32),
             pltpu.SMEM((1, LANES), jnp.int32),
-            pltpu.VMEM((3, 2, 4, PS, LANES), F32),
-            pltpu.VMEM((3, 2, 4, PS, LANES), F32),
+            pltpu.VMEM((3, 2, 4, PS // 2, LANES), F32),
+            pltpu.VMEM((3, 2, 4, PS // 2, LANES), F32),
             dma((WIDE,)),
             dma((WIDE,)),
             dma((STAGES, WIDE)),
@@ -383,14 +404,14 @@
     return pl.pallas_call(
         kernel,
         out_shape=jax.ShapeDtypeStruct((3, PS, PS, LANES), F32),
-        in_specs=[anywhere, anywhere, anywhere, vmem],
+        in_specs=[anywhere, anywhere, anywhere, pl.BlockSpec(memory_space=pltpu.SMEM)],
         out_specs=vmem,
         scratch_shapes=scratch,
         compiler_params=pltpu.CompilerParams(
             collective_id=0, has_side_effects=True, vmem_limit_bytes=60 << 20
         ),
         name="regrid_and_sweep",
-    )(fields, source, kappa, labels)
+    )(fields, source, kappa, patch_ids)
 
 
 def solution(mesh):

time: 167 us -> 164 us (0.982)
  no operation moved by 1% of the time
where the time goes in v5:
time: 164 us
  Pallas kernels  161 us (98%)
  local copies, waits for them, and re-layouts  2.67 us (2%)
    pallas_call x1, Pallas kernels, local(): pl.pallas_call(kernel, out_shape=jax.ShapeDtypeStruct((3, PS, PS, LANES),...  161 us

profile of v5, /device:TPU:40, one launch (start us, length us, event | category | flops | bytes accessed | tf_op | source)
XLA Modules:
  0.0 163.7 jit_solution(7998827490031939654)
XLA Ops:
  0.0 161.0 %regrid_and_sweep.1 = f32[3,32,32,128]{3,2,1,0:T(8,128)} custom-call(f32[3,2048,128]{2,1,0:T(8,128)} %bitcast.19, f32[3,2048,128]{2,1,0:T(8,128)} %bitcast.20, f32[2048,128]{1,0:T(8,128)} %bitcast.21, s32[8]{0:T(128)} %ids.1), custom_call_target="tpu_custom_call" | custom-call | tf_op jit(solution)/shard_map/regrid_and_sweep/pallas_call | solution.py:404
  161.0 2.7 %copy.6 = f32[3,32,32,128]{3,2,1,0:T(8,128)} copy(f32[3,32,32,128]{3,2,1,0:T(8,128)} %regrid_and_sweep.1) | data formatting | bytes 3145728
